TPU v7x, 32 devices: a whole 2x2x4 slice. The times are simulated.
32 devices in a mesh: seq: 4 (over y, core), batch: 8 (over z, x).
Axes of the slice: x: 2, y: 2, z: 4, core: 2. Of those that a mesh axis runs over, the one named last changes fastest.
Arguments:
- waveforms: bfloat16 [8, 24, 16000], P('batch', 'seq'), may hold values from -6 to 6
- clip_lengths: int32 [8, 4], P('batch'), may hold values from 1 to 6, as said below
- block_starts: int32 [8, 24], P('batch'), may hold values from 0 to 744, as said below
- conv_first: bfloat16 [384, 1280], P('batch'), may hold values from -0.3125 to 0.3125
- bias_first: float32 [1280], replicated, may hold values from -3 to 3
- conv_second: bfloat16 [3840, 1280], replicated, may hold values from -0.09375 to 0.09375
- bias_second: float32 [1280], replicated, may hold values from -3 to 3
- norm_gain: float32 [1280], replicated, may hold values from 0.25 to 1.75
- projector: bfloat16 [1280, 4096], P(None, 'seq'), may hold values from -0.15625 to 0.15625
- proj_bias: float32 [4096], P('seq'), may hold values from -3 to 3
Outputs:
- audio_rows: bfloat16 [8, 768, 4096], P('batch', 'seq')
Inputs may be any that keep to these rules, and one draw needn't show every extreme that they name: `clip_lengths`: the lengths of a sequence's 4 clips sum to 12, and one clip has 6 blocks. `block_starts`: A clip's live blocks start 24 positions apart, in slot order; live blocks of a sequence occupy disjoint positions; entries of dead slots are 0.
All inputs are finite; a program needn't handle non-finite values.
Results may differ from a plain program's by a relative error of at most 0.0055.
Values may be sent and summed in bfloat16 or wider, within the bound.
A program may use at most 64 MiB of HBM per device.

v0:
```python
import jax
import jax.numpy as jnp
import numpy as np
from jax import lax
from jax.sharding import PartitionSpec as P

MEL = 128
WIDTH = 1280
HOP = 160
WINDOW = 400
BINS = 201
FRAMES = 96
TOK = 24
OWN_ROWS = 192


def hertz_to_mel(hertz):
    return np.where(
        hertz < 1000.0,
        hertz / (200.0 / 3.0),
        15.0 + np.log(np.maximum(hertz, 1.0) / 1000.0) / (np.log(6.4) / 27.0),
    )


def mel_to_hertz(mels):
    return np.where(
        mels < 15.0, mels * 200.0 / 3.0, 1000.0 * np.exp((mels - 15.0) * np.log(6.4) / 27.0)
    )


def spectral_tables():
    sample_rate = HOP * 100.0
    sample_index = np.arange(WINDOW)
    hann = 0.5 - 0.5 * np.cos(2.0 * np.pi * sample_index / WINDOW)
    angles = 2.0 * np.pi * np.outer(sample_index, np.arange(BINS)) / WINDOW
    dft_basis = np.concatenate(
        [hann[:, None] * np.cos(angles), -hann[:, None] * np.sin(angles)], axis=1
    )
    edges = mel_to_hertz(
        np.linspace(0.0, float(hertz_to_mel(np.array(sample_rate / 2.0))), MEL + 2)
    )
    bin_hertz = np.arange(BINS) * sample_rate / WINDOW
    rising = (bin_hertz[:, None] - edges[None, :-2]) / (edges[1:-1] - edges[:-2])[None, :]
    falling = (edges[None, 2:] - bin_hertz[:, None]) / (edges[2:] - edges[1:-1])[None, :]
    filters = (
        np.maximum(0.0, np.minimum(rising, falling)) * (2.0 / (edges[2:] - edges[:-2]))[None, :]
    )
    return (jnp.asarray(dft_basis.astype(np.float32)), jnp.asarray(filters.astype(np.float32)))


def encode(blocks_in, tables, conv_first, bias_first, conv_second, bias_second, norm_gain):
    dft_basis, filters = tables
    block_count = blocks_in.shape[0]
    segments = blocks_in.astype(jnp.float32).reshape(block_count, FRAMES + 4, HOP)
    frames = jnp.concatenate(
        [
            segments[:, :FRAMES],
            segments[:, 1 : FRAMES + 1],
            segments[:, 2 : FRAMES + 2, : HOP // 2],
        ],
        axis=2,
    )
    frames = frames.reshape(block_count * FRAMES, WINDOW)
    spectrum = jnp.dot(frames, dft_basis, precision=lax.Precision.HIGHEST)
    power_bins = spectrum[:, :BINS] * spectrum[:, :BINS] + spectrum[:, BINS:] * spectrum[:, BINS:]
    energy = jnp.dot(power_bins, filters, precision=lax.Precision.HIGHEST)
    features = (
        ((jnp.log10(energy + 1e-10) + 4.0) / 4.0)
        .astype(jnp.bfloat16)
        .reshape(block_count, FRAMES, MEL)
    )
    zero_mel = jnp.zeros((block_count, 1, MEL), jnp.bfloat16)
    padded = jnp.concatenate([zero_mel, features, zero_mel], axis=1)
    stacked = jnp.concatenate([padded[:, :-2], padded[:, 1:-1], padded[:, 2:]], axis=2).reshape(
        block_count * FRAMES, 3 * MEL
    )
    hidden = jax.nn.gelu(
        jnp.dot(stacked, conv_first, preferred_element_type=jnp.float32) + bias_first,
        approximate=False,
    )
    hidden = hidden.astype(jnp.bfloat16).reshape(block_count, FRAMES // 2, 2, WIDTH)
    even_rows = hidden[:, :, 0]
    odd_rows = hidden[:, :, 1]
    before = jnp.concatenate(
        [jnp.zeros((block_count, 1, WIDTH), jnp.bfloat16), odd_rows[:, :-1]], axis=1
    )
    second_in = jnp.concatenate([before, even_rows, odd_rows], axis=2).reshape(
        block_count * FRAMES // 2, 3 * WIDTH
    )
    activated = jax.nn.gelu(
        jnp.dot(second_in, conv_second, preferred_element_type=jnp.float32) + bias_second,
        approximate=False,
    )
    pooled = jnp.mean(activated.reshape(block_count, TOK, 2, WIDTH), axis=2)
    row_mean = jnp.mean(pooled, axis=-1, keepdims=True)
    centred = pooled - row_mean
    row_var = jnp.mean(centred * centred, axis=-1, keepdims=True)
    normed = centred / jnp.sqrt(row_var + 1e-05) * norm_gain
    return normed.astype(jnp.bfloat16).reshape(block_count * TOK, WIDTH)


def shards(
    waveforms,
    clip_lengths,
    block_starts,
    conv_first,
    bias_first,
    conv_second,
    bias_second,
    norm_gain,
    projector,
    proj_bias,
):
    tables = spectral_tables()
    devices_seq = lax.axis_size("seq")
    slots_all = waveforms.shape[1]
    lengths = clip_lengths[0]
    starts = block_starts[0]
    whole_first = lax.all_gather(conv_first, "batch", axis=0, tiled=True)
    blocks = waveforms[0]
    group_slot = jnp.arange(devices_seq * slots_all, dtype=jnp.int32)
    group_live = group_slot % slots_all < jnp.repeat(lengths, slots_all)
    token_rows = encode(
        blocks, tables, whole_first, bias_first, conv_second, bias_second, norm_gain
    )
    projected = (
        jnp.dot(
            lax.all_gather(token_rows, "seq", axis=0, tiled=True),
            projector,
            preferred_element_type=jnp.float32,
        )
        + proj_bias
    ).astype(jnp.bfloat16)
    total_rows = projected.shape[0]
    length_all = devices_seq * OWN_ROWS
    offsets = jnp.arange(TOK, dtype=jnp.int32)
    target = jnp.where(group_live[:, None], starts[:, None] + offsets[None, :], length_all).reshape(
        -1
    )
    row_index = (
        jnp.full((length_all,), total_rows, jnp.int32)
        .at[target]
        .set(jnp.arange(total_rows, dtype=jnp.int32), mode="drop")
    )
    padded_rows = jnp.concatenate(
        [projected, jnp.zeros((1, projected.shape[1]), jnp.bfloat16)], axis=0
    )
    placed = jnp.take(padded_rows, row_index, axis=0)
    owned_rows = lax.all_to_all(placed, "seq", split_axis=0, concat_axis=1, tiled=True)
    return owned_rows[None]


def solution(mesh):
    return jax.shard_map(
        shards,
        mesh=mesh,
        in_specs=(
            P("batch", "seq", None),
            P("batch", None),
            P("batch", None),
            P("batch", None),
            P(),
            P(),
            P(),
            P(),
            P(None, "seq"),
            P("seq"),
        ),
        out_specs=P("batch", "seq", None),
        check_vma=False,
    )
```

profile of v0, /device:TPU:0, one launch (start us, length us, event | category | flops | bytes accessed | tf_op | source)
XLA Modules:
  0.0 152.7 jit_solution(5425280199517510005)
XLA Ops:
  6.5 1.5 reshape.141
  8.0 0.1 fusion.49
  8.1 0.0 copy-start.1
  8.2 0.5 pad_maximum_fusion
  8.6 0.0 copy-start.9
  8.6 0.6 copy-done.1
  9.3 2.4 %fusion.50 = f32[576,402]{0,1:T(8,128)S(1)} fusion(f32[576,400]{1,0:T(8,128)S(1)} %bitcast.32, f32[400,402]{1,0:T(8,128)S(1)} %copy-done.1), kind=kOutput, calls=%fused_computation.88 | convolution fusion | flops 1111449600 | bytes 2491008 | tf_op jit(solution)/shard_map/dot_general | solution.py:64
  11.7 0.0 copy-start.2
  11.7 0.0 copy-start.6
  11.7 1.2 fusion.30
  12.9 0.1 pad_slice_fusion.1
  13.0 34.7 %all_gather.6 = bf16[384,1280]{1,0:T(8,128)(2,1)S(1)} all-gather(bf16[48,1280]{1,0:T(8,128)(2,1)S(1)} %copy-done.2), channel_id=1, replica_groups=mesh['seq'=4,'batch'=8] {'batch'}, dimensions={0}, use_global_device_ids=true | all-gather | bytes 1105920 | tf_op jit(solution)/shard_map/all_gather | solution.py:119
  47.7 7.8 %fusion.2 = bf16[576,1280]{1,0:T(8,128)(2,1)} fusion(bf16[384,1280]{1,0:T(8,128)(2,1)S(1)} %all_gather.6, f32[1280]{0:T(1024)S(1)} %copy-done.6, bf16[576,128]{1,0:T(8,128)(2,1)S(1)} %bitcast.39, bf16[576,128]{1,0:T(8,128)(2,1)S(1)} %fusion.30, bf16[576,128]{1,0:T(8,128)(2,1)S(1)} %bitcast.38), kind=kOutput, calls=%fused_computation.6 | convolution fusion | flops 616218624 | bytes 2905088 | tf_op jit(solution)/shard_map/dot_general | solution.py:78
  55.5 4.3 %reshape.139 = bf16[6,48,2,1280]{3,2,1,0:T(2,128)(2,1)} reshape(bf16[576,1280]{1,0:T(8,128)(2,1)} %fusion.2) | data formatting | bytes 2949120 | tf_op jit(solution)/shard_map/reshape | solution.py:81
  59.8 4.3 %fusion.48 = (bf16[6,48,1,1280]{3,2,1,0:T(2,128)(2,1)S(1)}, bf16[6,48,1,1280]{3,2,1,0:T(2,128)(2,1)S(1)}) fusion(bf16[6,48,2,1280]{3,2,1,0:T(2,128)(2,1)} %reshape.139), kind=kLoop, calls=%fused_computation.86 | loop fusion | bytes 2949120 | tf_op jit(solution)/shard_map/slice | solution.py:82
  64.1 0.1 copy.23
  64.2 0.1 copy.20
  64.3 0.0 copy-start.7
  64.3 0.1 copy.21
  64.4 0.2 concatenate.40
  64.6 0.4 copy-done.7
  65.0 10.8 %fusion.16 = f32[288,1280]{1,0:T(8,128)} fusion(bf16[3840,1280]{1,0:T(8,128)(2,1)} %param.17, bf16[288,1280]{1,0:T(8,128)(2,1)S(1)} %bitcast.34, bf16[288,1280]{1,0:T(8,128)(2,1)S(1)} %bitcast.35, bf16[288,1280]{1,0:T(8,128)(2,1)S(1)} %bitcast.36, f32[1280]{0:T(1024)S(1)} %copy-done.7), kind=kOutput, calls=%fused_computation.32 | convolution fusion | flops 2861752320 | bytes 13521920 | tf_op jit(solution)/shard_map/dot_general | solution.py:91
  75.9 3.0 %reshape.140 = f32[6,24,2,1280]{3,2,1,0:T(2,128)} reshape(f32[288,1280]{1,0:T(8,128)} %fusion.16) | data formatting | bytes 2949120 | tf_op jit(solution)/shard_map/reshape | solution.py:94
  78.9 3.1 %reduce_sum.27 = f32[6,24,1280]{2,1,0:T(8,128)S(1)} reduce(f32[6,24,2,1280]{3,2,1,0:T(2,128)} %reshape.140, f32[]{:T(128)} %constant.65.clone.1), dimensions={2}, to_apply=%region_1.2 | reduce | flops 184320 | bytes 2211844 | tf_op jit(solution)/shard_map/reduce_sum | solution.py:94
  82.0 0.0 copy-start.3
  82.0 0.1 fusion.47
  82.1 0.0 copy-start.4
  82.2 0.0 copy-start.5
  82.2 0.0 copy-start.8
  82.2 0.9 multiply_reduce_fusion
  83.1 0.1 div.33
  83.2 0.1 sqrt.12
  83.3 2.0 %fusion.33 = bf16[144,1280]{1,0:T(8,128)(2,1)} fusion(f32[6,24,1280]{2,1,0:T(8,128)} %get-tuple-element.8, f32[1280]{0:T(1024)S(1)} %copy-done.3, f32[144]{0:T(256)S(1)} %sqrt.12, f32[144]{0:T(256)S(1)} %div.33), kind=kLoop, calls=%fused_computation.58 | loop fusion | flops 737280 | bytes 1112192 | tf_op jit(solution)/shard_map/convert_element_type | solution.py:99
  85.3 0.0 all-gather.2.cloned.1.call-update
  85.3 0.1 broadcast_in_dim.50
  85.4 0.1 reshape.136
  85.5 0.1 add_select_fusion
  85.6 0.1 select_n.48
  85.7 4.1 %scatter_custom_fusion = s32[768]{0:T(1024)S(1)} fusion(s32[576]{0:T(1024)S(1)} %fusion.41, s32[576]{0:T(1024)S(1)} %iota.13, s32[]{:T(128)} %constant.45.clone.1), kind=kCustom, calls=%fused_computation.79 | custom fusion | bytes 3076 | tf_op jit(solution)/shard_map/scatter | solution.py:143
  89.8 0.1 broadcast_in_dim.54
  89.9 15.4 %all-gather.2.cloned.1.call-done = bf16[576,1280]{1,0:T(8,128)(2,1)} async-done(((bf16[144,1280]{1,0:T(8,128)(2,1)}), bf16[576,1280]{1,0:T(8,128)(2,1)}) %all-gather.2.cloned.1.call-update) | async-done | bytes 1474576 | tf_op jit(solution)/shard_map/all_gather | solution.py:128
  105.3 3.1 %add_convert_fusion = bf16[576,1024]{1,0:T(8,128)(2,1)S(1)} fusion(bf16[576,1280]{1,0:T(8,128)(2,1)} %all-gather.2.cloned.1.call-done, bf16[1280,1024]{1,0:T(8,128)(2,1)S(1)} %copy-done, f32[1024]{0:T(1024)S(1)} %copy-done.8), kind=kOutput, calls=%fused_computation.23 | convolution fusion | flops 1511129088 | bytes 5279744 | tf_op jit(solution)/shard_map/dot_general | solution.py:127
  108.4 1.1 concatenate.45
  109.5 6.0 %gather_fusion = bf16[768,1024]{1,0:T(8,128)(2,1)} fusion(bf16[577,1024]{1,0:T(8,128)(2,1)} %concatenate.45, s32[1024]{0:T(1024)S(1)} %pad_clamp_fusion), kind=kCustom, calls=%fused_computation | custom fusion | bytes 3148800 | tf_op jit(solution)/shard_map/jit(_take)/gather | solution.py:148
  115.5 1.6 %broadcast_select_fusion = bf16[4,192,1024]{2,1,0:T(8,128)(2,1)S(1)} fusion(bf16[4,192,1024]{2,1,0:T(8,128)(2,1)} %bitcast.31, pred[4,192]{1,0:T(4,128)(4,1)S(1)} %broadcast_in_dim.54), kind=kLoop, calls=%fused_computation.30 | loop fusion | flops 786432 | bytes 3146496 | tf_op jit(solution)/shard_map/jit(_take)/select_n | solution.py:148
  117.1 22.5 %all_to_all.13 = bf16[4,192,1024]{2,1,0:T(8,128)(2,1)S(1)} all-to-all(bf16[4,192,1024]{2,1,0:T(8,128)(2,1)S(1)} %broadcast_select_fusion), channel_id=1, replica_groups=mesh['seq'=4,'batch'=8] {'seq'}, dimensions={0} | all-to-all | bytes 3145728 | tf_op jit(solution)/shard_map/all_to_all | solution.py:149
  139.6 2.4 %copy.19 = bf16[192,4,1024]{2,1,0:T(4,128)(2,1)} copy(bf16[192,4,1024]{2,0,1:T(8,128)(2,1)S(1)} %bitcast.30) | data formatting | bytes 3145728 | tf_op jit(solution)/shard_map/all_to_all | solution.py:149
  142.0 3.8 %broadcast_in_dim.58 = bf16[1,192,4096]{2,1,0:T(8,128)(2,1)} reshape(bf16[192,4,1024]{2,1,0:T(4,128)(2,1)} %copy.19) | data formatting | bytes 3145728 | tf_op jit(solution)/shard_map/broadcast_in_dim | solution.py:150
  (19 shorter events, 0.1 us)
Async XLA Ops:
  6.5 98.8 %copy-start = (bf16[1280,1024]{1,0:T(8,128)(2,1)S(1)}, bf16[1280,1024]{1,0:T(8,128)(2,1)}, u32[]{:S(2)}) copy-start(bf16[1280,1024]{1,0:T(8,128)(2,1)} %param.20) | copy-start | bytes 7864324
  6.5 98.8 %all-gather.2.cloned.1.call-start = ((), (), s32[]{:S(2)}) async-start(), calls=%async_computation.1 | async-start | bytes 1843200 | tf_op jit(solution)/shard_map/all_gather | solution.py:128
  8.1 1.1 copy-start.1
  8.6 3.0 %copy-start.9 = (f32[201,128]{1,0:T(8,128)S(1)}, f32[201,128]{1,0:T(8,128)}, u32[]{:S(2)}) copy-start(f32[201,128]{1,0:T(8,128)} %constant.21.clone) | copy-start | bytes 308740
  11.7 1.3 copy-start.2
  11.7 36.0 %copy-start.6 = (f32[1280]{0:T(1024)S(1)}, f32[1280]{0:T(1024)}, u32[]{:S(2)}) copy-start(f32[1280]{0:T(1024)} %param.16) | copy-start | bytes 15364
  64.3 0.7 copy-start.7
  82.0 1.3 copy-start.3
  82.1 3.2 %copy-start.4 = (s32[1,4]{1,0:T(1,128)S(1)}, s32[1,4]{1,0:T(1,128)}, u32[]{:S(2)}) copy-start(s32[1,4]{1,0:T(1,128)} %param.13) | copy-start | bytes 52
  82.2 3.4 %copy-start.5 = (s32[1,24]{1,0:T(1,128)S(1)}, s32[1,24]{1,0:T(1,128)}, u32[]{:S(2)}) copy-start(s32[1,24]{1,0:T(1,128)} %param.14) | copy-start | bytes 292
  82.2 23.2 %copy-start.8 = (f32[1024]{0:T(1024)S(1)}, f32[1024]{0:T(1024)}, u32[]{:S(2)}) copy-start(f32[1024]{0:T(1024)} %param.21) | copy-start | bytes 12292
Sparse Core Ops, SparseCore 0:
  85.5 19.8 all-gather.1
where the time goes:
time: 153 us
  blocking collectives  57.2 us (37%)
  local copies, waits for them, and re-layouts  32.6 us (21%)
  matrix products  25.3 us (17%)
  waiting for transfers between devices  15.4 us (10%)
  between operations  13.7 us (9%)
  other arithmetic  8.41 us (5%)
    all_gather x1, blocking collectives, shards(): whole_first = lax.all_gather(conv_first, 'batch', axis=0, tiled=True)  34.7 us
    all_to_all x1, blocking collectives, shards(): lax.all_to_all(placed, 'seq', split_axis=0, concat_axis=1, tiled=True)  22.5 us
    all_gather x1, waiting for transfers between devices, shards(): lax.all_gather(token_rows, 'seq', axis=0, tiled=True)  15.4 us
    dot_general x1, matrix products, encode(): jnp.dot(second_in, conv_second, preferred_element_type=jnp.float32)  10.8 us
    dot_general x1, matrix products, encode(): jnp.dot(stacked, conv_first, preferred_element_type=jnp.float32)  7.85 us
    gather x1, local copies, waits for them, and re-layouts, shards(): placed = jnp.take(padded_rows, row_index, axis=0)  5.97 us
    reshape x1, local copies, waits for them, and re-layouts, encode(): hidden.astype(jnp.bfloat16).reshape(block_count, FRAMES // 2, 2, WIDTH)  4.31 us
    slice x1, local copies, waits for them, and re-layouts, encode(): even_rows = hidden[:, :, 0]  4.28 us
  transfers between devices with their start and end apart: 1, of which 1 were waited for; matrix products, arithmetic and copies ran while one was open for 3% of the time, Pallas kernels for 0%

commit v1 on v0

v1 whole, which is shorter than its diff:
```python
import functools

import jax
import jax.numpy as jnp
import ml_dtypes
import numpy as np
from jax import lax
from jax.experimental import pallas as pl
from jax.experimental.pallas import tpu as pltpu
from jax.sharding import PartitionSpec as P

MEL = 128
WIDTH = 1280
HOP = 160
WINDOW = 400
BINS = 201
TOK = 24
OWN_ROWS = 192
W = 3
ROWS = W * TOK
HALF = WIDTH // 2
CHUNK = 256
SEGS = 25
SEG = 4 * HOP
PIECES = 2
MESH = pl.DeviceIdType.MESH


def hertz_to_mel(hertz):
    return np.where(
        hertz < 1000.0,
        hertz / (200.0 / 3.0),
        15.0 + np.log(np.maximum(hertz, 1.0) / 1000.0) / (np.log(6.4) / 27.0),
    )


def mel_to_hertz(mels):
    return np.where(
        mels < 15.0, mels * 200.0 / 3.0, 1000.0 * np.exp((mels - 15.0) * np.log(6.4) / 27.0)
    )


def spectral_tables():
    sample_rate = HOP * 100.0
    sample_index = np.arange(WINDOW)
    hann = 0.5 - 0.5 * np.cos(2.0 * np.pi * sample_index / WINDOW)
    angles = 2.0 * np.pi * np.outer(sample_index, np.arange(BINS)) / WINDOW
    basis = np.zeros((512, 512), np.float32)
    basis[:WINDOW, :BINS] = hann[:, None] * np.cos(angles)
    basis[:WINDOW, 256 : 256 + BINS] = -hann[:, None] * np.sin(angles)
    edges = mel_to_hertz(
        np.linspace(0.0, float(hertz_to_mel(np.array(sample_rate / 2.0))), MEL + 2)
    )
    bin_hertz = np.arange(BINS) * sample_rate / WINDOW
    rising = (bin_hertz[:, None] - edges[None, :-2]) / (edges[1:-1] - edges[:-2])[None, :]
    falling = (edges[None, 2:] - bin_hertz[:, None]) / (edges[2:] - edges[1:-1])[None, :]
    filters = np.zeros((256, MEL), np.float32)
    filters[:BINS] = (
        np.maximum(0.0, np.minimum(rising, falling)) * (2.0 / (edges[2:] - edges[:-2]))[None, :]
    )
    terms = []
    rest = basis
    for _ in range(3):
        term = rest.astype(ml_dtypes.bfloat16)
        terms.append(term)
        rest = rest - term.astype(np.float32)
    return jnp.asarray(np.stack(terms)), jnp.asarray(filters)


def gelu(x):
    return 0.5 * x * (1.0 + lax.erf(x * np.float32(np.sqrt(0.5))))


def shift_rows(x, by):
    rows = x.shape[0]
    moved = pltpu.roll(x, by % rows, axis=0)
    place = lax.broadcasted_iota(jnp.int32, (rows, 1), 0) % TOK
    edge = 0 if by == 1 else TOK - 1
    return jnp.where(place == edge, 0.0, moved)


def kernel(
    n_seq,
    n_batch,
    slots,
    lengths_ref,
    starts_ref,
    waves_hbm,
    first_hbm,
    bias1_ref,
    second_hbm,
    bias2_ref,
    gain_ref,
    projector_hbm,
    pbias_ref,
    basis_hbm,
    filters_ref,
    out_ref,
    waves,
    first,
    second,
    projector,
    basis,
    conv_in,
    pooled,
    tokens,
    placed,
    local_sem,
    wave_send,
    wave_recv,
    first_send,
    first_recv,
    tok_send,
    tok_recv,
    out_send,
    out_recv,
):
    me = lax.axis_index("seq")
    row = lax.axis_index("batch")
    core = lax.rem(me, 2)
    chip = lax.div(me, 2)
    n_chip = n_seq // 2
    partner = chip * 2 + (1 - core)
    cols = projector.shape[1]
    piece = cols // PIECES

    def across(k):
        return lax.rem(chip + k, n_chip) * 2 + core

    def source(k):
        return lax.rem(chip - k + n_chip, n_chip) * 2 + core

    def peer(k):
        return lax.rem(row + k, n_batch)

    loads = [
        pltpu.make_async_copy(waves_hbm, waves.at[pl.ds(me * slots, slots)], local_sem.at[0]),
        pltpu.make_async_copy(basis_hbm, basis, local_sem.at[1]),
        pltpu.make_async_copy(first_hbm, first.at[row], local_sem.at[2]),
        pltpu.make_async_copy(second_hbm, second, local_sem.at[3]),
        pltpu.make_async_copy(projector_hbm, projector, local_sem.at[4]),
    ]
    for load in loads:
        load.start()

    barrier = pltpu.get_barrier_semaphore()
    pl.semaphore_signal(barrier, inc=1, device_id=(partner, row), device_id_type=MESH)
    for k in range(1, n_chip):
        pl.semaphore_signal(barrier, inc=1, device_id=(across(k), row), device_id_type=MESH)
    for k in range(1, n_batch):
        pl.semaphore_signal(barrier, inc=1, device_id=(me, peer(k)), device_id_type=MESH)
    pl.semaphore_wait(barrier, n_chip + n_batch - 1)

    def gather(own, place, send, recv):
        copies = []
        for k in range(n_chip):
            target = partner if k == 0 else across(k)
            copies.append(
                pltpu.make_async_remote_copy(
                    src_ref=own,
                    dst_ref=place(me),
                    send_sem=send.at[k],
                    recv_sem=recv.at[k],
                    device_id=(target, row),
                    device_id_type=MESH,
                )
            )
        return copies

    def relay(place, send, recv):
        return [
            pltpu.make_async_remote_copy(
                src_ref=place(source(k)),
                dst_ref=place(source(k)),
                send_sem=send.at[n_chip - 1 + k],
                recv_sem=recv.at[n_chip - 1 + k],
                device_id=(partner, row),
                device_id_type=MESH,
            )
            for k in range(1, n_chip)
        ]

    def wave_place(s):
        return waves.at[pl.ds(s * slots, slots)]

    wave_copies = gather(waves_hbm, wave_place, wave_send, wave_recv)
    wave_relays = relay(wave_place, wave_send, wave_recv)
    for copy in wave_copies[1:] + wave_copies[:1]:
        copy.start()

    half = pl.ds(pl.multiple_of(core * HALF, 128), HALF)
    first_copies = []
    first_relays = []
    for k in range(1, n_batch):
        first_copies.append(
            pltpu.make_async_remote_copy(
                src_ref=first_hbm.at[:, half],
                dst_ref=first.at[row, :, half],
                send_sem=first_send.at[k - 1],
                recv_sem=first_recv.at[k - 1],
                device_id=(me, peer(k)),
                device_id_type=MESH,
            )
        )
        origin = lax.rem(row - k + n_batch, n_batch)
        first_relays.append(
            pltpu.make_async_remote_copy(
                src_ref=first.at[origin, :, half],
                dst_ref=first.at[origin, :, half],
                send_sem=first_send.at[n_batch - 2 + k],
                recv_sem=first_recv.at[n_batch - 2 + k],
                device_id=(partner, row),
                device_id_type=MESH,
            )
        )
    for copy in first_copies:
        copy.start()

    for k in range(1, n_chip):
        wave_copies[k].wait_recv()
        wave_relays[k - 1].start()
    wave_copies[0].wait_recv()
    for copy in wave_relays:
        copy.wait_recv()
    loads[0].wait()

    ends = []
    total = 0
    for d in range(n_seq):
        total = total + lengths_ref[0, d]
        ends.append(total)

    def live_slot(j):
        slot = j
        for d in range(n_seq - 1):
            slot = slot + jnp.where(j >= ends[d], slots - lengths_ref[0, d], 0)
        return jnp.clip(slot, 0, n_seq * slots - 1)

    pieces = []
    for i in range(W):
        block = waves[live_slot(me * W + i)].astype(jnp.float32)
        pieces.append(jnp.concatenate([block[: SEGS - 1], block[1:, :256]], axis=1))
    samples = jnp.concatenate(pieces, axis=0)
    frames = [samples[:, :512]]
    for r in range(1, 4):
        wide = samples[:, 128 * r : min(128 * r + 640, 896)]
        frames.append(pltpu.roll(wide, wide.shape[1] - 32 * r, axis=1)[:, :512])
    frames = jnp.concatenate(frames, axis=0).astype(jnp.bfloat16)
    loads[1].wait()
    spectrum = jnp.dot(frames, basis[2], preferred_element_type=jnp.float32)
    spectrum += jnp.dot(frames, basis[1], preferred_element_type=jnp.float32)
    spectrum += jnp.dot(frames, basis[0], preferred_element_type=jnp.float32)
    real, imag = spectrum[:, :256], spectrum[:, 256:]
    power = real * real + imag * imag
    energy = jnp.dot(
        power,
        filters_ref[...],
        precision=lax.Precision.HIGHEST,
        preferred_element_type=jnp.float32,
    )
    features = (jnp.log(energy + 1e-10) * np.float32(1.0 / np.log(10.0)) + 4.0) * 0.25
    feat = [features[r * ROWS : (r + 1) * ROWS] for r in range(4)]
    stacked = jnp.concatenate(
        [
            jnp.concatenate([shift_rows(feat[3], 1)] + feat[:3], axis=0),
            features,
            jnp.concatenate(feat[1:] + [shift_rows(feat[0], -1)], axis=0),
        ],
        axis=1,
    ).astype(jnp.bfloat16)

    for k in range(n_batch - 1):
        first_copies[k].wait_recv()
        first_relays[k].start()
    for copy in first_relays:
        copy.wait_recv()
    loads[2].wait()

    @pl.loop(0, WIDTH // CHUNK)
    def _(n):
        at = pl.ds(pl.multiple_of(n * CHUNK, CHUNK), CHUNK)
        weight = first[:, :, at].reshape(3 * MEL, CHUNK)
        hidden = gelu(
            jnp.dot(stacked, weight, preferred_element_type=jnp.float32) + bias1_ref[:, at]
        )
        hid = [hidden[r * ROWS : (r + 1) * ROWS] for r in range(4)]
        taps = [[shift_rows(hid[3], 1), hid[1]], [hid[0], hid[2]], [hid[1], hid[3]]]
        for t in range(3):
            to = pl.ds(pl.multiple_of(t * WIDTH + n * CHUNK, CHUNK), CHUNK)
            conv_in[:, to] = jnp.concatenate(taps[t], axis=0).astype(jnp.bfloat16)

    loads[3].wait()

    @pl.loop(0, WIDTH // CHUNK)
    def _(n):
        at = pl.ds(pl.multiple_of(n * CHUNK, CHUNK), CHUNK)
        activated = gelu(
            jnp.dot(conv_in[...], second[:, at], preferred_element_type=jnp.float32)
            + bias2_ref[:, at]
        )
        pooled[:, at] = (activated[:ROWS] + activated[ROWS:]) * 0.5

    whole = pooled[...]
    centred = whole - jnp.mean(whole, axis=1, keepdims=True)
    variance = jnp.mean(centred * centred, axis=1, keepdims=True)
    normed = centred / jnp.sqrt(variance + 1e-05) * gain_ref[...]
    tokens[me] = jnp.concatenate([normed[:, :HALF], normed[:, HALF:]], axis=0).astype(jnp.bfloat16)

    def tok_place(s):
        return tokens.at[s]

    tok_copies = gather(tokens.at[me], tok_place, tok_send, tok_recv)
    tok_relays = relay(tok_place, tok_send, tok_recv)
    for copy in tok_copies[1:] + tok_copies[:1]:
        copy.start()
    tok_copies[0].wait_recv()
    loads[4].wait()

    def group_rows(g):
        pair = [tokens[g * 2 + c].astype(jnp.float32) for c in range(2)]
        left = jnp.concatenate([p[:ROWS] for p in pair], axis=0).astype(jnp.bfloat16)
        right = jnp.concatenate([p[ROWS:] for p in pair], axis=0).astype(jnp.bfloat16)
        return left, right

    out_copies = []
    out_relays = []
    for k in range(n_chip):
        g = lax.rem(chip - k + n_chip, n_chip)
        if k > 0:
            tok_copies[k].wait_recv()
            tok_relays[k - 1].start()
            tok_relays[k - 1].wait_recv()
        left, right = group_rows(g)
        for h in range(PIECES):
            at = slice(h * piece, (h + 1) * piece)
            value = jnp.dot(left, projector[:HALF, at], preferred_element_type=jnp.float32)
            value += jnp.dot(right, projector[HALF:, at], preferred_element_type=jnp.float32)
            placed[k, h, me] = (value + pbias_ref[:, at]).astype(jnp.bfloat16)

            step = []
            for j in range(n_chip):
                target = partner if j == 0 else across(j)
                step.append(
                    pltpu.make_async_remote_copy(
                        src_ref=placed.at[k, h, me],
                        dst_ref=placed.at[(k + j) % n_chip, h, me],
                        send_sem=out_send.at[k, h, j],
                        recv_sem=out_recv.at[k, h, j],
                        device_id=(target, row),
                        device_id_type=MESH,
                    )
                )
            for copy in step[1:] + step[:1]:
                copy.start()
            out_copies.append((k, h, step))
            out_relays.append(
                [
                    pltpu.make_async_remote_copy(
                        src_ref=placed.at[(k + j) % n_chip, h, source(j)],
                        dst_ref=placed.at[(k + j) % n_chip, h, source(j)],
                        send_sem=out_send.at[k, h, n_chip - 1 + j],
                        recv_sem=out_recv.at[k, h, n_chip - 1 + j],
                        device_id=(partner, row),
                        device_id_type=MESH,
                    )
                    for j in range(1, n_chip)
                ]
            )

    span = 2 * ROWS
    column = lax.broadcasted_iota(jnp.int32, (1, span), 1)
    position = lax.broadcasted_iota(jnp.int32, (OWN_ROWS, 1), 0) + me * OWN_ROWS
    hots = []
    for k in range(n_chip):
        g = lax.rem(chip - k + n_chip, n_chip)
        goal = column
        for i in range(2 * W):
            begin = starts_ref[0, live_slot(g * 2 * W + i)] - i * TOK
            goal = goal + jnp.where(lax.div(column, TOK) == i, begin, 0)
        hots.append(jnp.where(position == goal, 1.0, 0.0).astype(jnp.bfloat16))

    def place(h, s):
        value = jnp.dot(hots[0], placed[0, h, s], preferred_element_type=jnp.float32)
        for k in range(1, n_chip):
            value += jnp.dot(hots[k], placed[k, h, s], preferred_element_type=jnp.float32)
        to = pl.ds(pl.multiple_of(s * cols + h * piece, 128), piece)
        out_ref[:, to] = value.astype(jnp.bfloat16)

    for (k, h, step), relays in zip(out_copies, out_relays):
        for j in range(1, n_chip):
            step[j].wait_recv()
            relays[j - 1].start()
        if k == n_chip - 1:
            place(h, me)
    for k, h, step in out_copies:
        step[0].wait_recv()
        if k == n_chip - 1:
            place(h, partner)
    for relays in out_relays:
        for copy in relays:
            copy.wait_recv()
    for h in range(PIECES):
        for j in range(1, n_chip):
            place(h, source(j))
            place(h, source(j) + 1 - 2 * core)

    for copy in wave_copies + wave_relays + first_copies + first_relays + tok_copies + tok_relays:
        copy.wait_send()
    for (k, h, step), relays in zip(out_copies, out_relays):
        for copy in step + relays:
            copy.wait_send()


def shards(
    waveforms,
    clip_lengths,
    block_starts,
    conv_first,
    bias_first,
    conv_second,
    bias_second,
    norm_gain,
    projector,
    proj_bias,
):
    basis, filters = spectral_tables()
    n_seq = lax.axis_size("seq")
    n_batch = lax.axis_size("batch")
    n_chip = n_seq // 2
    slots = waveforms.shape[1]
    cols = projector.shape[1]
    piece = cols // PIECES
    hops = 2 * n_chip - 1
    anywhere = pl.BlockSpec(memory_space=pl.ANY)
    vmem = pl.BlockSpec(memory_space=pltpu.VMEM)
    smem = pl.BlockSpec(memory_space=pltpu.SMEM)
    dma = pltpu.SemaphoreType.DMA
    bf16 = jnp.bfloat16
    out = pl.pallas_call(
        functools.partial(kernel, n_seq, n_batch, slots),
        out_shape=jax.ShapeDtypeStruct((OWN_ROWS, n_seq * cols), bf16),
        in_specs=[
            smem,
            smem,
            anywhere,
            anywhere,
            vmem,
            anywhere,
            vmem,
            vmem,
            anywhere,
            vmem,
            anywhere,
            vmem,
        ],
        out_specs=vmem,
        scratch_shapes=[
            pltpu.VMEM((n_seq * slots, SEGS, SEG), bf16),
            pltpu.VMEM((n_batch,) + conv_first.shape, bf16),
            pltpu.VMEM(conv_second.shape, bf16),
            pltpu.VMEM(projector.shape, bf16),
            pltpu.VMEM(basis.shape, bf16),
            pltpu.VMEM((2 * ROWS, 3 * WIDTH), bf16),
            pltpu.VMEM((ROWS, WIDTH), jnp.float32),
            pltpu.VMEM((n_seq, 2 * ROWS, HALF), bf16),
            pltpu.VMEM((n_chip, PIECES, n_seq, 2 * ROWS, piece), bf16),
            dma((5,)),
            dma((hops,)),
            dma((hops,)),
            dma((2 * n_batch - 2,)),
            dma((2 * n_batch - 2,)),
            dma((hops,)),
            dma((hops,)),
            dma((n_chip, PIECES, hops)),
            dma((n_chip, PIECES, hops)),
        ],
        compiler_params=pltpu.CompilerParams(
            collective_id=0, has_side_effects=True, vmem_limit_bytes=60 * 1024 * 1024
        ),
        name="encoder",
    )(
        clip_lengths,
        block_starts,
        waveforms.reshape(slots, SEGS, SEG),
        conv_first,
        bias_first.reshape(1, -1),
        conv_second,
        bias_second.reshape(1, -1),
        norm_gain.reshape(1, -1),
        projector,
        proj_bias.reshape(1, -1),
        basis,
        filters,
    )
    return out[None]


def solution(mesh):
    return jax.shard_map(
        shards,
        mesh=mesh,
        in_specs=(
            P("batch", "seq", None),
            P("batch", None),
            P("batch", None),
            P("batch", None),
            P(),
            P(),
            P(),
            P(),
            P(None, "seq"),
            P("seq"),
        ),
        out_specs=P("batch", "seq", None),
        check_vma=False,
    )
```

time: 153 us -> 53.3 us (0.35)
  the two profiles are of different devices: /device:TPU:0 before, /device:TPU:11 now
where the time goes in v1:
time: 53.3 us; the launch traced here: 53 us
  Pallas kernels  44.4 us (83%)
  local copies, waits for them, and re-layouts  8.52 us (16%)
    pallas_call x1, Pallas kernels, shards(): pl.pallas_call(functools.partial(kernel, n_seq, n_batch, slots), out_shap...  44.4 us
    unnamed x1, local copies, waits for them, and re-layouts  2.7 us
    reshape x1, local copies, waits for them, and re-layouts, shards(): waveforms.reshape(slots, SEGS, SEG)  1.94 us
    reshape x1, local copies, waits for them, and re-layouts, shards(): bias_second.reshape(1, -1)  1.3 us
    reshape x1, local copies, waits for them, and re-layouts, shards(): bias_first.reshape(1, -1)  1.29 us
    reshape x1, local copies, waits for them, and re-layouts, shards(): norm_gain.reshape(1, -1)  1.29 us

profile of v1, /device:TPU:11, one launch (start us, length us, event | category | flops | bytes accessed | tf_op | source)
XLA Modules:
  0.0 53.0 jit_solution(15860541068528638368)
XLA Ops:
  0.0 1.3 %reshape.16.bias1_ref = f32[1,1280]{1,0:T(1,128)} reshape(f32[1280]{0:T(1024)} %param.16) | data formatting | bytes 10240 | tf_op jit(solution)/shard_map/reshape | solution.py:486
  1.3 1.3 %reshape.17.bias2_ref = f32[1,1280]{1,0:T(1,128)} reshape(f32[1280]{0:T(1024)} %param.18) | data formatting | bytes 10240 | tf_op jit(solution)/shard_map/reshape | solution.py:488
  2.6 1.3 %reshape.18.gain_ref = f32[1,1280]{1,0:T(1,128)} reshape(f32[1280]{0:T(1024)} %param.19) | data formatting | bytes 10240 | tf_op jit(solution)/shard_map/reshape | solution.py:489
  3.9 1.9 %reshape.15.waves_hbm = bf16[6,25,640]{2,1,0:T(8,128)(2,1)} reshape(bf16[1,6,16000]{2,1,0:T(8,128)(2,1)} %param.12) | data formatting | bytes 384000 | tf_op jit(solution)/shard_map/reshape | solution.py:484
  5.8 44.4 %encoder.1 = bf16[192,4096]{1,0:T(8,128)(2,1)} custom-call(s32[1,4]{1,0:T(1,128)} %lengths_ref.1, s32[1,24]{1,0:T(1,128)} %starts_ref.1, bf16[6,25,640]{2,1,0:T(8,128)(2,1)} %reshape.15.waves_hbm, bf16[48,1280]{1,0:T(8,128)(2,1)} %first_hbm.1, f32[1,1280]{1,0:T(1,128)} %reshape.16.bias1_ref, bf16[3840,1280]{1,0:T(8,128)(2,1)} %second_hbm.1, ...), custom_call_target="tpu_custom_call" | custom-call | tf_op jit(solution)/shard_map/encoder/pallas_call | solution.py:439
  50.3 2.7 %copy.14 = bf16[1,192,4096]{2,1,0:T(8,128)(2,1)} copy(bf16[1,192,4096]{2,1,0:T(8,128)(2,1)} %bitcast.2) | data formatting | bytes 3145728

commit v2 on v1

--- a/solution.py
+++ b/solution.py
@@ -22,8 +22,9 @@
 CHUNK = 256
 SEGS = 25
 SEG = 4 * HOP
-PIECES = 2
+PARTS = 4
 MESH = pl.DeviceIdType.MESH
+VMEM_MIB = 48
 
 
 def hertz_to_mel(hertz):
@@ -83,19 +84,23 @@
     n_seq,
     n_batch,
     slots,
+    lengths_hbm,
+    starts_hbm,
+    waves_hbm,
+    first_hbm,
+    bias1_hbm,
+    second_hbm,
+    bias2_hbm,
+    gain_hbm,
+    projector_hbm,
+    pbias_hbm,
+    basis_hbm,
+    filters_hbm,
+    out_ref,
     lengths_ref,
     starts_ref,
-    waves_hbm,
-    first_hbm,
-    bias1_ref,
-    second_hbm,
-    bias2_ref,
-    gain_ref,
-    projector_hbm,
     pbias_ref,
-    basis_hbm,
     filters_ref,
-    out_ref,
     waves,
     first,
     second,
@@ -105,6 +110,11 @@
     pooled,
     tokens,
     placed,
+    bias1_ref,
+    bias2_ref,
+    gain_ref,
+    extra,
+    extra_bias,
     local_sem,
     wave_send,
     wave_recv,
@@ -114,6 +124,8 @@
     tok_recv,
     out_send,
     out_recv,
+    extra_send,
+    extra_recv,
 ):
     me = lax.axis_index("seq")
     row = lax.axis_index("batch")
@@ -122,7 +134,7 @@
     n_chip = n_seq // 2
     partner = chip * 2 + (1 - core)
     cols = projector.shape[1]
-    piece = cols // PIECES
+    n_pieces, n_far, piece = split(n_chip, cols)
 
     def across(k):
         return lax.rem(chip + k, n_chip) * 2 + core
@@ -134,13 +146,20 @@
         return lax.rem(row + k, n_batch)
 
     loads = [
-        pltpu.make_async_copy(waves_hbm, waves.at[pl.ds(me * slots, slots)], local_sem.at[0]),
+        pltpu.make_async_copy(waves_hbm, waves.at[me], local_sem.at[0]),
         pltpu.make_async_copy(basis_hbm, basis, local_sem.at[1]),
         pltpu.make_async_copy(first_hbm, first.at[row], local_sem.at[2]),
         pltpu.make_async_copy(second_hbm, second, local_sem.at[3]),
         pltpu.make_async_copy(projector_hbm, projector, local_sem.at[4]),
+        pltpu.make_async_copy(bias1_hbm, bias1_ref.at[0], local_sem.at[5]),
+        pltpu.make_async_copy(bias2_hbm, bias2_ref.at[0], local_sem.at[6]),
+        pltpu.make_async_copy(gain_hbm, gain_ref.at[0], local_sem.at[7]),
+        pltpu.make_async_copy(pbias_hbm, pbias_ref.at[0], local_sem.at[8]),
+        pltpu.make_async_copy(filters_hbm, filters_ref, local_sem.at[9]),
+        pltpu.make_async_copy(lengths_hbm, lengths_ref, local_sem.at[10]),
+        pltpu.make_async_copy(starts_hbm, starts_ref, local_sem.at[11]),
     ]
-    for load in loads:
+    for load in loads[:1] + loads[2:3] + loads[1:2] + loads[5:] + loads[3:5]:
         load.start()
 
     barrier = pltpu.get_barrier_semaphore()
@@ -181,7 +200,7 @@
         ]
 
     def wave_place(s):
-        return waves.at[pl.ds(s * slots, slots)]
+        return waves.at[s]
 
     wave_copies = gather(waves_hbm, wave_place, wave_send, wave_recv)
     wave_relays = relay(wave_place, wave_send, wave_recv)
@@ -216,6 +235,53 @@
     for copy in first_copies:
         copy.start()
 
+    lane = lax.rem(row, 2)
+    beside = row + 1 - 2 * lane
+    part = WIDTH // PARTS
+    extra_copies = []
+    extra_relays = []
+    if n_far < n_pieces:
+        from_col = pl.multiple_of((n_far + lane) * piece, 128)
+        for i in range(PARTS):
+            at = pl.ds(i * part, part)
+            extra_copies.append(
+                pltpu.make_async_remote_copy(
+                    src_ref=projector_hbm.at[at, pl.ds(from_col, piece)],
+                    dst_ref=extra.at[lane, at],
+                    send_sem=extra_send.at[i],
+                    recv_sem=extra_recv.at[i],
+                    device_id=(across(1), row),
+                    device_id_type=MESH,
+                )
+            )
+            extra_relays.append(
+                pltpu.make_async_remote_copy(
+                    src_ref=extra.at[lane, at],
+                    dst_ref=extra.at[lane, at],
+                    send_sem=extra_send.at[PARTS + i],
+                    recv_sem=extra_recv.at[PARTS + i],
+                    device_id=(me, beside),
+                    device_id_type=MESH,
+                )
+            )
+        extra_copies.append(
+            pltpu.make_async_remote_copy(
+                src_ref=pbias_hbm,
+                dst_ref=extra_bias.at[0],
+                send_sem=extra_send.at[2 * PARTS],
+                recv_sem=extra_recv.at[2 * PARTS],
+                device_id=(across(1), row),
+                device_id_type=MESH,
+            )
+        )
+        for copy in extra_copies:
+            copy.start()
+
+    def pass_on(i):
+        if extra_relays:
+            extra_copies[i].wait_recv()
+            extra_relays[i].start()
+
     for k in range(1, n_chip):
         wave_copies[k].wait_recv()
         wave_relays[k - 1].start()
@@ -223,6 +289,8 @@
     for copy in wave_relays:
         copy.wait_recv()
     loads[0].wait()
+    for load in loads[9:]:
+        load.wait()
 
     ends = []
     total = 0
@@ -231,14 +299,22 @@
         ends.append(total)
 
     def live_slot(j):
-        slot = j
+        device, slot = 0, j
         for d in range(n_seq - 1):
-            slot = slot + jnp.where(j >= ends[d], slots - lengths_ref[0, d], 0)
-        return jnp.clip(slot, 0, n_seq * slots - 1)
+            past = j >= ends[d]
+            device = device + jnp.where(past, 1, 0)
+            slot = slot - jnp.where(past, lengths_ref[0, d], 0)
+        return device, jnp.clip(slot, 0, slots - 1)
 
     pieces = []
     for i in range(W):
-        block = waves[live_slot(me * W + i)].astype(jnp.float32)
+        device, slot = live_slot(me * W + i)
+        clip = waves[device].astype(jnp.float32)
+        mine = lax.broadcasted_iota(jnp.int32, (slots, 1), 0) == slot
+        line = jnp.sum(jnp.where(mine, clip, 0.0), axis=0, keepdims=True)
+        block = jnp.concatenate(
+            [line[:, q * SEG : (q + 1) * SEG] for q in range(SEGS)], axis=0
+        )
         pieces.append(jnp.concatenate([block[: SEGS - 1], block[1:, :256]], axis=1))
     samples = jnp.concatenate(pieces, axis=0)
     frames = [samples[:, :512]]
@@ -272,23 +348,30 @@
     for k in range(n_batch - 1):
         first_copies[k].wait_recv()
         first_relays[k].start()
-    for copy in first_relays:
-        copy.wait_recv()
     loads[2].wait()
-
-    @pl.loop(0, WIDTH // CHUNK)
-    def _(n):
-        at = pl.ds(pl.multiple_of(n * CHUNK, CHUNK), CHUNK)
-        weight = first[:, :, at].reshape(3 * MEL, CHUNK)
+    loads[5].wait()
+    pass_on(0)
+
+    def first_half(begin):
+        at = pl.ds(pl.multiple_of(begin, 128), HALF)
+        weight = first[:, :, at].reshape(3 * MEL, HALF)
         hidden = gelu(
             jnp.dot(stacked, weight, preferred_element_type=jnp.float32) + bias1_ref[:, at]
         )
         hid = [hidden[r * ROWS : (r + 1) * ROWS] for r in range(4)]
         taps = [[shift_rows(hid[3], 1), hid[1]], [hid[0], hid[2]], [hid[1], hid[3]]]
         for t in range(3):
-            to = pl.ds(pl.multiple_of(t * WIDTH + n * CHUNK, CHUNK), CHUNK)
+            to = pl.ds(pl.multiple_of(t * WIDTH + begin, 128), HALF)
             conv_in[:, to] = jnp.concatenate(taps[t], axis=0).astype(jnp.bfloat16)
 
+    first_half(core * HALF)
+    for copy in first_relays:
+        copy.wait_recv()
+    first_half((1 - core) * HALF)
+    pass_on(1)
+
+    loads[6].wait()
+    loads[7].wait()
     loads[3].wait()
 
     @pl.loop(0, WIDTH // CHUNK)
@@ -300,6 +383,7 @@
         )
         pooled[:, at] = (activated[:ROWS] + activated[ROWS:]) * 0.5
 
+    pass_on(2)
     whole = pooled[...]
     centred = whole - jnp.mean(whole, axis=1, keepdims=True)
     variance = jnp.mean(centred * centred, axis=1, keepdims=True)
@@ -313,8 +397,10 @@
     tok_relays = relay(tok_place, tok_send, tok_recv)
     for copy in tok_copies[1:] + tok_copies[:1]:
         copy.start()
+    pass_on(3)
     tok_copies[0].wait_recv()
     loads[4].wait()
+    loads[8].wait()
 
     def group_rows(g):
         pair = [tokens[g * 2 + c].astype(jnp.float32) for c in range(2)]
@@ -322,50 +408,72 @@
         right = jnp.concatenate([p[ROWS:] for p in pair], axis=0).astype(jnp.bfloat16)
         return left, right
 
-    out_copies = []
-    out_relays = []
+    def project(rows, weight, bias):
+        value = jnp.dot(rows[0], weight[:HALF], preferred_element_type=jnp.float32)
+        value += jnp.dot(rows[1], weight[HALF:], preferred_element_type=jnp.float32)
+        return (value + bias).astype(jnp.bfloat16)
+
+    def far_slot(k, j):
+        return (k + j) % n_chip
+
+    steps = {}
+    relays = {}
+    for k in range(n_chip):
+        for h in range(n_pieces):
+            steps[k, h] = [
+                pltpu.make_async_remote_copy(
+                    src_ref=placed.at[k, h, me],
+                    dst_ref=placed.at[far_slot(k, j), h, me],
+                    send_sem=out_send.at[k, h, j],
+                    recv_sem=out_recv.at[k, h, j],
+                    device_id=(partner if j == 0 else across(j), row),
+                    device_id_type=MESH,
+                )
+                for j in range(n_chip if h < n_far else 1)
+            ]
+            relays[k, h] = [
+                pltpu.make_async_remote_copy(
+                    src_ref=placed.at[far_slot(k, j), h, source(j)],
+                    dst_ref=placed.at[far_slot(k, j), h, source(j)],
+                    send_sem=out_send.at[k, h, n_chip - 1 + j],
+                    recv_sem=out_recv.at[k, h, n_chip - 1 + j],
+                    device_id=(partner, row),
+                    device_id_type=MESH,
+                )
+                for j in range(1, n_chip)
+            ]
+
+    def own_piece(k, h, rows):
+        at = slice(h * piece, (h + 1) * piece)
+        placed[k, h, me] = project(rows, projector[:, at], pbias_ref[:, at])
+        for copy in steps[k, h][1:] + steps[k, h][:1]:
+            copy.start()
+
+    grouped = []
     for k in range(n_chip):
         g = lax.rem(chip - k + n_chip, n_chip)
         if k > 0:
             tok_copies[k].wait_recv()
             tok_relays[k - 1].start()
             tok_relays[k - 1].wait_recv()
-        left, right = group_rows(g)
-        for h in range(PIECES):
-            at = slice(h * piece, (h + 1) * piece)
-            value = jnp.dot(left, projector[:HALF, at], preferred_element_type=jnp.float32)
-            value += jnp.dot(right, projector[HALF:, at], preferred_element_type=jnp.float32)
-            placed[k, h, me] = (value + pbias_ref[:, at]).astype(jnp.bfloat16)
-
-            step = []
-            for j in range(n_chip):
-                target = partner if j == 0 else across(j)
-                step.append(
-                    pltpu.make_async_remote_copy(
-                        src_ref=placed.at[k, h, me],
-                        dst_ref=placed.at[(k + j) % n_chip, h, me],
-                        send_sem=out_send.at[k, h, j],
-                        recv_sem=out_recv.at[k, h, j],
-                        device_id=(target, row),
-                        device_id_type=MESH,
-                    )
+        grouped.append(group_rows(g))
+        for h in range(n_far):
+            own_piece(k, h, grouped[k])
+    for k in range(n_chip):
+        for h in range(n_far, n_pieces):
+            own_piece(k, h, grouped[k])
+    if extra_relays:
+        extra_copies[PARTS].wait_recv()
+        for copy in extra_relays:
+            copy.wait_recv()
+        for k in range(n_chip):
+            for h in range(n_far, n_pieces):
+                at = slice(h * piece, (h + 1) * piece)
+                to = far_slot(k, 1)
+                placed[to, h, source(1)] = project(
+                    grouped[to], extra[h - n_far], extra_bias[:, at]
                 )
-            for copy in step[1:] + step[:1]:
-                copy.start()
-            out_copies.append((k, h, step))
-            out_relays.append(
-                [
-                    pltpu.make_async_remote_copy(
-                        src_ref=placed.at[(k + j) % n_chip, h, source(j)],
-                        dst_ref=placed.at[(k + j) % n_chip, h, source(j)],
-                        send_sem=out_send.at[k, h, n_chip - 1 + j],
-                        recv_sem=out_recv.at[k, h, n_chip - 1 + j],
-                        device_id=(partner, row),
-                        device_id_type=MESH,
-                    )
-                    for j in range(1, n_chip)
-                ]
-            )
+                relays[k, h][0].start()
 
     span = 2 * ROWS
     column = lax.broadcasted_iota(jnp.int32, (1, span), 1)
@@ -375,7 +483,8 @@
         g = lax.rem(chip - k + n_chip, n_chip)
         goal = column
         for i in range(2 * W):
-            begin = starts_ref[0, live_slot(g * 2 * W + i)] - i * TOK
+            device, slot = live_slot(g * 2 * W + i)
+            begin = starts_ref[0, device * slots + slot] - i * TOK
             goal = goal + jnp.where(lax.div(column, TOK) == i, begin, 0)
         hots.append(jnp.where(position == goal, 1.0, 0.0).astype(jnp.bfloat16))
 
@@ -386,29 +495,44 @@
         to = pl.ds(pl.multiple_of(s * cols + h * piece, 128), piece)
         out_ref[:, to] = value.astype(jnp.bfloat16)
 
-    for (k, h, step), relays in zip(out_copies, out_relays):
-        for j in range(1, n_chip):
-            step[j].wait_recv()
-            relays[j - 1].start()
-        if k == n_chip - 1:
-            place(h, me)
-    for k, h, step in out_copies:
-        step[0].wait_recv()
-        if k == n_chip - 1:
-            place(h, partner)
-    for relays in out_relays:
-        for copy in relays:
-            copy.wait_recv()
-    for h in range(PIECES):
+    for h in range(n_pieces):
+        place(h, me)
+    for k in range(n_chip):
+        for h in range(n_pieces):
+            steps[k, h][0].wait_recv()
+    for h in range(n_pieces):
+        place(h, partner)
+    for k in range(n_chip):
+        for h in range(n_far):
+            for j in range(1, n_chip):
+                steps[k, h][j].wait_recv()
+                relays[k, h][j - 1].start()
+    for h in reversed(range(n_pieces)):
         for j in range(1, n_chip):
             place(h, source(j))
+    for k in range(n_chip):
+        for h in range(n_pieces):
+            for copy in relays[k, h]:
+                copy.wait_recv()
+    for h in range(n_pieces):
+        for j in range(1, n_chip):
             place(h, source(j) + 1 - 2 * core)
 
     for copy in wave_copies + wave_relays + first_copies + first_relays + tok_copies + tok_relays:
         copy.wait_send()
-    for (k, h, step), relays in zip(out_copies, out_relays):
-        for copy in step + relays:
+    for copy in extra_copies + extra_relays:
+        copy.wait_send()
+    for key in steps:
+        for copy in steps[key]:
             copy.wait_send()
+        for copy in relays[key]:
+            copy.wait_send()
+
+
+def split(n_chip, cols):
+    if n_chip == 2 and cols % 512 == 0:
+        return 4, 2, cols // 4
+    return 2, 2, cols // 2
 
 
 def shards(
@@ -429,33 +553,23 @@
     n_chip = n_seq // 2
     slots = waveforms.shape[1]
     cols = projector.shape[1]
-    piece = cols // PIECES
+    n_pieces, _, piece = split(n_chip, cols)
     hops = 2 * n_chip - 1
-    anywhere = pl.BlockSpec(memory_space=pl.ANY)
+    hbm = pl.BlockSpec(memory_space=pltpu.HBM)
     vmem = pl.BlockSpec(memory_space=pltpu.VMEM)
-    smem = pl.BlockSpec(memory_space=pltpu.SMEM)
     dma = pltpu.SemaphoreType.DMA
     bf16 = jnp.bfloat16
     out = pl.pallas_call(
         functools.partial(kernel, n_seq, n_batch, slots),
         out_shape=jax.ShapeDtypeStruct((OWN_ROWS, n_seq * cols), bf16),
-        in_specs=[
-            smem,
-            smem,
-            anywhere,
-            anywhere,
-            vmem,
-            anywhere,
-            vmem,
-            vmem,
-            anywhere,
-            vmem,
-            anywhere,
-            vmem,
-        ],
+        in_specs=[hbm] * 12,
         out_specs=vmem,
         scratch_shapes=[
-            pltpu.VMEM((n_seq * slots, SEGS, SEG), bf16),
+            pltpu.SMEM(clip_lengths.shape, jnp.int32),
+            pltpu.SMEM(block_starts.shape, jnp.int32),
+            pltpu.VMEM((1, cols), jnp.float32),
+            pltpu.VMEM(filters.shape, jnp.float32),
+            pltpu.VMEM((n_seq, slots, SEGS * SEG), bf16),
             pltpu.VMEM((n_batch,) + conv_first.shape, bf16),
             pltpu.VMEM(conv_second.shape, bf16),
             pltpu.VMEM(projector.shape, bf16),
@@ -463,34 +577,46 @@
             pltpu.VMEM((2 * ROWS, 3 * WIDTH), bf16),
             pltpu.VMEM((ROWS, WIDTH), jnp.float32),
             pltpu.VMEM((n_seq, 2 * ROWS, HALF), bf16),
-            pltpu.VMEM((n_chip, PIECES, n_seq, 2 * ROWS, piece), bf16),
-            dma((5,)),
+            pltpu.VMEM((n_chip, n_pieces, n_seq, 2 * ROWS, piece), bf16),
+            pltpu.VMEM((1, WIDTH), jnp.float32),
+            pltpu.VMEM((1, WIDTH), jnp.float32),
+            pltpu.VMEM((1, WIDTH), jnp.float32),
+            pltpu.VMEM((2, WIDTH, piece), bf16),
+            pltpu.VMEM((1, cols), jnp.float32),
+            dma((12,)),
             dma((hops,)),
             dma((hops,)),
             dma((2 * n_batch - 2,)),
             dma((2 * n_batch - 2,)),
             dma((hops,)),
             dma((hops,)),
-            dma((n_chip, PIECES, hops)),
-            dma((n_chip, PIECES, hops)),
+            dma((n_chip, n_pieces, hops)),
+            dma((n_chip, n_pieces, hops)),
+            dma((2 * PARTS + 1,)),
+            dma((2 * PARTS + 1,)),
         ],
         compiler_params=pltpu.CompilerParams(
-            collective_id=0, has_side_effects=True, vmem_limit_bytes=60 * 1024 * 1024
+            collective_id=0, has_side_effects=True, vmem_limit_bytes=VMEM_MIB * 1024 * 1024
         ),
         name="encoder",
     )(
-        clip_lengths,
-        block_starts,
-        waveforms.reshape(slots, SEGS, SEG),
-        conv_first,
-        bias_first.reshape(1, -1),
-        conv_second,
-        bias_second.reshape(1, -1),
-        norm_gain.reshape(1, -1),
-        projector,
-        proj_bias.reshape(1, -1),
-        basis,
-        filters,
+        *[
+            pltpu.with_memory_space_constraint(x, pltpu.HBM)
+            for x in (
+                clip_lengths,
+                block_starts,
+                waveforms.reshape(slots, SEGS * SEG),
+                conv_first,
+                bias_first,
+                conv_second,
+                bias_second,
+                norm_gain,
+                projector,
+                proj_bias,
+                basis,
+                filters,
+            )
+        ]
     )
     return out[None]
 

time: 53.3 us -> 42.7 us (0.80)
  the two profiles are of different devices: /device:TPU:11 before, /device:TPU:0 now
where the time goes in v2:
time: 42.7 us; the launch traced here: 42.6 us
  Pallas kernels  41.4 us (97%)
  local copies, waits for them, and re-layouts  1.15 us (3%)
    pallas_call x1, Pallas kernels, shards(): pl.pallas_call(functools.partial(kernel, n_seq, n_batch, slots), out_shap...  41.4 us
    unnamed x1, local copies, waits for them, and re-layouts  1.15 us

profile of v2, /device:TPU:0, one launch (start us, length us, event | category | flops | bytes accessed | tf_op | source)
XLA Modules:
  0.0 42.6 jit_solution(3037375201936832020)
XLA Ops:
  0.0 41.4 %encoder.1 = bf16[192,4096]{1,0:T(8,128)(2,1)S(1)} custom-call(s32[1,4]{1,0:T(1,128)} %lengths_hbm.1, s32[1,24]{1,0:T(1,128)} %starts_hbm.1, bf16[6,16000]{1,0:T(8,128)(2,1)} %bitcast.3, bf16[48,1280]{1,0:T(8,128)(2,1)} %first_hbm.1, f32[1280]{0:T(1024)} %bias1_hbm.1, bf16[3840,1280]{1,0:T(8,128)(2,1)} %second_hbm.1, f32[1280]{0:T(1024)} %bias2_hbm.1, ...), custom_call_target="tpu_custom_call" | custom-call | tf_op jit(solution)/shard_map/encoder/pallas_call | solution.py:562
  41.4 1.1 %copy.14 = bf16[1,192,4096]{2,1,0:T(8,128)(2,1)} copy(bf16[1,192,4096]{2,1,0:T(8,128)(2,1)S(1)} %bitcast.2) | data formatting | bytes 3145728
